TPU v7x, 32 devices: a whole 2x2x4 slice. The times are simulated.
32 devices in a mesh: dp: 16 (over z, y, x), tensor: 2 (over core).
Axes of the slice: x: 2, y: 2, z: 4, core: 2. Of those that a mesh axis runs over, the one named last changes fastest.
Arguments:
- tokens: bfloat16 [16384, 768], P('dp'), may hold values from -6 to 6
- cotangent: bfloat16 [16384, 768], P('dp'), may hold values from -6 to 6
- lengths: int32 [32], P('dp'), may hold values from 113 to 512, as said below
- proj_weight: float32 [2, 768, 3, 768], P(None, 'dp', None, 'tensor'), may hold values from -0.21875 to 0.21875
- out_weight: float32 [2, 768, 768], P(None, 'dp', 'tensor'), may hold values from -0.875 to 0.875
- up_weight: float32 [2, 768, 3072], P(None, 'dp', 'tensor'), may hold values from -0.21875 to 0.21875
- down_weight: float32 [2, 768, 3072], P(None, 'dp', 'tensor'), may hold values from -0.109375 to 0.109375
- small_params: float32 [2, 8448], replicated, may hold values from -0.8 to 1.4
- proj_first: float32 [2, 768, 3, 768], P(None, 'dp', None, 'tensor'), may hold values from -0.00018310547 to 0.00018310547
- proj_second: float32 [2, 768, 3, 768], P(None, 'dp', None, 'tensor'), may hold values from 3.527916e-11 to 3.52791626e-09
- out_first: float32 [2, 768, 768], P(None, 'dp', 'tensor'), may hold values from -0.00018310547 to 0.00018310547
- out_second: float32 [2, 768, 768], P(None, 'dp', 'tensor'), may hold values from 7.0558325e-12 to 7.0558325e-10
- up_first: float32 [2, 768, 3072], P(None, 'dp', 'tensor'), may hold values from -0.00018310547 to 0.00018310547
- up_second: float32 [2, 768, 3072], P(None, 'dp', 'tensor'), may hold values from 3.527916e-11 to 3.52791626e-09
- down_first: float32 [2, 768, 3072], P(None, 'dp', 'tensor'), may hold values from -0.00018310547 to 0.00018310547
- down_second: float32 [2, 768, 3072], P(None, 'dp', 'tensor'), may hold values from 3.527916e-11 to 3.52791626e-09
- small_first: float32 [2, 8448], replicated, may hold values from -0.00018310547 to 0.00018310547
- small_second: float32 [2, 8448], replicated, may hold values from 3.527916e-11 to 5.644666e-10
Outputs:
- activations: float32 [16384, 768], P('dp')
- input_grad: float32 [16384, 768], P('dp')
- grad_norm: float32 [], replicated
- proj_first_new: float32 [2, 768, 3, 768], P(None, 'dp', None, 'tensor')
- proj_second_new: float32 [2, 768, 3, 768], P(None, 'dp', None, 'tensor')
- proj_weight_new: float32 [2, 768, 3, 768], P(None, 'dp', None, 'tensor')
- out_first_new: float32 [2, 768, 768], P(None, 'dp', 'tensor')
- out_second_new: float32 [2, 768, 768], P(None, 'dp', 'tensor')
- out_weight_new: float32 [2, 768, 768], P(None, 'dp', 'tensor')
- up_first_new: float32 [2, 768, 3072], P(None, 'dp', 'tensor')
- up_second_new: float32 [2, 768, 3072], P(None, 'dp', 'tensor')
- up_weight_new: float32 [2, 768, 3072], P(None, 'dp', 'tensor')
- down_first_new: float32 [2, 768, 3072], P(None, 'dp', 'tensor')
- down_second_new: float32 [2, 768, 3072], P(None, 'dp', 'tensor')
- down_weight_new: float32 [2, 768, 3072], P(None, 'dp', 'tensor')
- small_first_new: float32 [2, 8448], replicated
- small_second_new: float32 [2, 8448], replicated
- small_params_new: float32 [2, 8448], replicated
Inputs may be any that keep to these rules, and one draw needn't show every extreme that they name: `lengths`: each length is 512, 256 or 128, reduced by less than max(1, 16); the first sequence has length 512.
All inputs are finite; a program needn't handle non-finite values.
Results may differ from a plain program's by a relative error of at most 0.03.
The roundings to bfloat16 on the way count: a program that leaves them out, or rounds other values in their place, can miss the bound.
Values may be sent and summed in bfloat16 or wider, within the bound.
No kernel may reach another device: no remote copies, remote signals or barrier semaphores. Data moves between devices by JAX's collectives and lax.ppermute only.
A program may use at most 192 MiB of HBM per device.

v0:
```python
from functools import partial
import math
import jax
import jax.numpy as jnp
from jax import lax
from jax.sharding import PartitionSpec as P

D = 768
HEADS = 12
FF = 3072
beta_one = 0.9
beta_two = 0.999
adam_eps = 1e-06
decay_rate = 0.01
matrix_rate = 1.0
vector_rate = 0.3
clip_norm = 1.0
step_count = 10.0
norm_eps = 1e-06
masked_score = -1e30


def layer_norm(values, norm_gain, norm_shift):
    average = jnp.mean(values, axis=-1, keepdims=True)
    centered = values - average
    variance = jnp.mean(centered * centered, axis=-1, keepdims=True)
    return centered * lax.rsqrt(variance + norm_eps) * norm_gain + norm_shift


def split_vector(packed):
    bounds = [0, D, 2 * D, 2 * D + FF, 3 * D + FF, 4 * D + FF, 5 * D + FF, 6 * D + FF, 7 * D + FF]
    return [packed[bounds[place] : bounds[place + 1]] for place in range(8)]


def head_scores(query, keys, score_scale):
    return jnp.einsum("qhe,khe->hqk", query, keys, preferred_element_type=jnp.float32) * score_scale


def total_scores(pairs, score_scale):
    score_total = head_scores(pairs[0], pairs[1], score_scale)
    for place in range(2, len(pairs), 2):
        score_total = score_total + head_scores(pairs[place], pairs[place + 1], score_scale)
    return score_total


def attend_forward(block_item, score_scale):
    key_valid, value_rows = (block_item[0], block_item[1])
    score_total = total_scores(block_item[2:], score_scale)
    masked = jnp.where(key_valid[None, None, :], score_total, masked_score)
    row_max = jnp.max(masked, axis=-1, keepdims=True)
    exp_terms = jnp.exp(masked - row_max)
    row_sum = jnp.sum(exp_terms, axis=-1, keepdims=True)
    soft_low = (exp_terms / row_sum).astype(jnp.bfloat16)
    context = jnp.einsum("hqk,khe->qhe", soft_low, value_rows, preferred_element_type=jnp.float32)
    return (context.astype(jnp.bfloat16), (row_max + jnp.log(row_sum))[..., 0])


def attend_backward(block_item, score_scale, with_later, keep_total):
    key_valid, value_rows, log_norm, context_grad = (
        block_item[0],
        block_item[1],
        block_item[2],
        block_item[3],
    )
    rest = block_item[4:]
    if with_later:
        later = rest[0]
        pairs = rest[1:]
    else:
        pairs = rest
    score_total = total_scores(pairs, score_scale)
    soft = jnp.where(key_valid[None, None, :], jnp.exp(score_total - log_norm[..., None]), 0.0)
    soft_grad = jnp.einsum(
        "qhe,khe->hqk", context_grad, value_rows, preferred_element_type=jnp.float32
    )
    total_grad = soft * (soft_grad - jnp.sum(soft * soft_grad, axis=-1, keepdims=True))
    if with_later:
        total_grad = total_grad + later
    total_low = total_grad.astype(jnp.bfloat16)
    query_grad = (
        jnp.einsum("hqk,khe->qhe", total_low, pairs[1], preferred_element_type=jnp.float32)
        * score_scale
    )
    key_grad = (
        jnp.einsum("hqk,qhe->khe", total_low, pairs[0], preferred_element_type=jnp.float32)
        * score_scale
    )
    value_grad = jnp.einsum(
        "hqk,qhe->khe", soft.astype(jnp.bfloat16), context_grad, preferred_element_type=jnp.float32
    )
    results = (query_grad, key_grad, value_grad)
    if keep_total:
        results = results + (total_grad,)
    return results


def adam_parts(gradient, first, second, factor):
    clipped = gradient * factor
    first_new = beta_one * first + (1.0 - beta_one) * clipped
    second_new = beta_two * second + (1.0 - beta_two) * clipped * clipped
    first_hat = first_new / (1.0 - beta_one**step_count)
    second_hat = second_new / (1.0 - beta_two**step_count)
    return (first_new, second_new, first_hat / (jnp.sqrt(second_hat) + adam_eps))


def local(
    tokens,
    cotangent,
    lengths,
    proj_weight,
    out_weight,
    up_weight,
    down_weight,
    small_params,
    proj_first,
    proj_second,
    out_first,
    out_second,
    up_first,
    up_second,
    down_first,
    down_second,
    small_first,
    small_second,
):
    layers = proj_weight.shape[0]
    seq_count = lengths.shape[0]
    seq_len = tokens.shape[0] // seq_count
    local_width = proj_weight.shape[3]
    head_dim = D // HEADS
    local_heads = local_width // head_dim
    hidden_local = up_weight.shape[2]
    score_scale = 1.0 / math.sqrt(head_dim)
    share_scale = 1.0 / lax.axis_size("tensor")
    tensor_rank = lax.axis_index("tensor")
    proj_full, out_full, up_full, down_full = (
        lax.all_gather(proj_weight.astype(jnp.bfloat16), "dp", axis=1, tiled=True),
        lax.all_gather(out_weight.astype(jnp.bfloat16), "dp", axis=1, tiled=True),
        lax.all_gather(up_weight.astype(jnp.bfloat16), "dp", axis=1, tiled=True),
        lax.all_gather(down_weight.astype(jnp.bfloat16), "dp", axis=1, tiled=True),
    )
    positions = jnp.arange(seq_len)
    key_valid = positions[None, :] < lengths[:, None]
    row_valid = key_valid.reshape(-1, 1)

    def own_part(vector, width):
        return lax.dynamic_slice_in_dim(vector, tensor_rank * width, width)

    def place_part(local_values, full_width):
        return lax.dynamic_update_slice_in_dim(
            jnp.zeros((full_width,), jnp.float32),
            local_values,
            tensor_rank * local_values.shape[0],
            0,
        )

    def heads_view(rows):
        return rows.reshape(seq_count, seq_len, local_heads, head_dim)

    hidden = tokens.astype(jnp.float32)
    saved = []
    for layer_at in range(layers):
        bias_v, bias_o, bias_up, bias_down, gain_one, shift_one, gain_two, shift_two = split_vector(
            small_params[layer_at]
        )
        input_low = hidden.astype(jnp.bfloat16)
        projected = jnp.einsum(
            "td,dcf->tcf", input_low, proj_full[layer_at], preferred_element_type=jnp.float32
        )
        query_low = projected[:, 0].astype(jnp.bfloat16)
        key_low = projected[:, 1].astype(jnp.bfloat16)
        value_low = (projected[:, 2] + own_part(bias_v, local_width)).astype(jnp.bfloat16)
        pairs = [heads_view(query_low), heads_view(key_low)]
        for earlier in reversed(saved):
            pairs += [heads_view(earlier["query"]), heads_view(earlier["keys"])]
        context_low, log_norm = lax.map(
            partial(attend_forward, score_scale=score_scale),
            (key_valid, heads_view(value_low)) + tuple(pairs),
        )
        context_low = context_low.reshape(-1, local_width)
        attended = lax.psum(
            jnp.einsum(
                "tf,df->td", context_low, out_full[layer_at], preferred_element_type=jnp.float32
            ).astype(jnp.bfloat16),
            "tensor",
        ).astype(jnp.float32)
        first_in = hidden + attended + bias_o
        first_out = layer_norm(first_in, gain_one, shift_one)
        first_low = first_out.astype(jnp.bfloat16)
        before_act = jnp.einsum(
            "td,df->tf", first_low, up_full[layer_at], preferred_element_type=jnp.float32
        ) + own_part(bias_up, hidden_local)
        act_low = jax.nn.gelu(before_act, approximate=False).astype(jnp.bfloat16)
        returned = lax.psum(
            jnp.einsum(
                "tf,df->td", act_low, down_full[layer_at], preferred_element_type=jnp.float32
            ).astype(jnp.bfloat16),
            "tensor",
        ).astype(jnp.float32)
        second_in = first_out + returned + bias_down
        saved.append(
            {
                "layer_input": input_low,
                "query": query_low,
                "keys": key_low,
                "value_rows": value_low,
                "log_norm": log_norm,
                "context": context_low,
                "first_in": first_in,
                "first_low": first_low,
                "before_act": before_act,
                "act_low": act_low,
                "second_in": second_in,
            }
        )
        hidden = layer_norm(second_in, gain_two, shift_two)
    grad_rows = jnp.where(row_valid, cotangent.astype(jnp.float32), 0.0)
    proj_grads = [None] * layers
    out_grads = [None] * layers
    up_grads = [None] * layers
    down_grads = [None] * layers
    small_grads = [None] * layers
    later_total = None
    for layer_at in reversed(range(layers)):
        kept = saved[layer_at]
        bias_v, bias_o, bias_up, bias_down, gain_one, shift_one, gain_two, shift_two = split_vector(
            small_params[layer_at]
        )
        second_in_grad, gain_two_grad, shift_two_grad = jax.vjp(
            layer_norm, kept["second_in"], gain_two, shift_two
        )[1](grad_rows)
        down_in_low = second_in_grad.astype(jnp.bfloat16)
        down_grads[layer_at] = jnp.einsum(
            "td,tf->df", down_in_low, kept["act_low"], preferred_element_type=jnp.float32
        )
        act_grad = jnp.einsum(
            "td,df->tf", down_in_low, down_full[layer_at], preferred_element_type=jnp.float32
        )
        before_grad = jax.vjp(partial(jax.nn.gelu, approximate=False), kept["before_act"])[1](
            act_grad
        )[0]
        before_low = before_grad.astype(jnp.bfloat16)
        up_grads[layer_at] = jnp.einsum(
            "td,tf->df", kept["first_low"], before_low, preferred_element_type=jnp.float32
        )
        first_back = lax.psum(
            jnp.einsum(
                "tf,df->td", before_low, up_full[layer_at], preferred_element_type=jnp.float32
            ).astype(jnp.bfloat16),
            "tensor",
        ).astype(jnp.float32)
        first_out_grad = second_in_grad + first_back
        first_in_grad, gain_one_grad, shift_one_grad = jax.vjp(
            layer_norm, kept["first_in"], gain_one, shift_one
        )[1](first_out_grad)
        out_in_low = first_in_grad.astype(jnp.bfloat16)
        out_grads[layer_at] = jnp.einsum(
            "td,tf->df", out_in_low, kept["context"], preferred_element_type=jnp.float32
        )
        context_grad = jnp.einsum(
            "td,df->tf", out_in_low, out_full[layer_at], preferred_element_type=jnp.float32
        ).astype(jnp.bfloat16)
        pairs = [heads_view(kept["query"]), heads_view(kept["keys"])]
        for earlier in reversed(saved[:layer_at]):
            pairs += [heads_view(earlier["query"]), heads_view(earlier["keys"])]
        items = (
            key_valid,
            heads_view(kept["value_rows"]),
            kept["log_norm"],
            heads_view(context_grad),
        )
        with_later = later_total is not None
        if with_later:
            items = items + (later_total,)
        items = items + tuple(pairs)
        results = lax.map(
            partial(
                attend_backward,
                score_scale=score_scale,
                with_later=with_later,
                keep_total=layer_at > 0,
            ),
            items,
        )
        later_total = results[3] if layer_at > 0 else None
        query_grad = results[0].reshape(-1, local_width)
        key_grad = results[1].reshape(-1, local_width)
        value_grad = results[2].reshape(-1, local_width)
        proj_grad_low = jnp.stack([query_grad, key_grad, value_grad], axis=1).astype(jnp.bfloat16)
        proj_grads[layer_at] = jnp.einsum(
            "td,tcf->dcf", kept["layer_input"], proj_grad_low, preferred_element_type=jnp.float32
        )
        input_back = lax.psum(
            jnp.einsum(
                "tcf,dcf->td",
                proj_grad_low,
                proj_full[layer_at],
                preferred_element_type=jnp.float32,
            ).astype(jnp.bfloat16),
            "tensor",
        ).astype(jnp.float32)
        grad_rows = first_in_grad + input_back
        small_grads[layer_at] = jnp.concatenate(
            [
                place_part(jnp.sum(value_grad, axis=0), D),
                share_scale * jnp.sum(first_in_grad, axis=0),
                place_part(jnp.sum(before_grad, axis=0), FF),
                share_scale * jnp.sum(second_in_grad, axis=0),
                share_scale * gain_one_grad,
                share_scale * shift_one_grad,
                share_scale * gain_two_grad,
                share_scale * shift_two_grad,
            ]
        )
    big_totals = (
        jnp.stack(proj_grads),
        jnp.stack(out_grads),
        jnp.stack(up_grads),
        jnp.stack(down_grads),
    )
    small_partial = jnp.stack(small_grads)
    row_count = proj_weight.shape[1]
    summed = lax.psum((big_totals[0], big_totals[1], big_totals[2], big_totals[3]), "dp")
    row_start = lax.axis_index("dp") * row_count
    shares = tuple(
        (lax.dynamic_slice_in_dim(summed_part, row_start, row_count, 1) for summed_part in summed)
    )
    masters = (proj_weight, out_weight, up_weight, down_weight)
    firsts = (proj_first, out_first, up_first, down_first)
    seconds = (proj_second, out_second, up_second, down_second)
    square_part = jnp.sum(shares[0] * shares[0])
    for kind_at in range(1, 4):
        square_part = square_part + jnp.sum(shares[kind_at] * shares[kind_at])
    weight_square = jnp.stack(
        [jnp.sum(master * master, axis=tuple(range(1, master.ndim))) for master in masters]
    )
    square_big, weight_square, small_grad = lax.psum(
        (square_part, weight_square, small_partial), ("dp", "tensor")
    )
    grad_norm = jnp.sqrt(square_big + jnp.sum(small_grad * small_grad))
    factor = clip_norm / jnp.maximum(grad_norm, clip_norm)
    moments = []
    updates = []
    for kind_at in range(4):
        first_new, second_new, direction = adam_parts(
            shares[kind_at], firsts[kind_at], seconds[kind_at], factor
        )
        moments.append((first_new, second_new))
        updates.append(direction + decay_rate * masters[kind_at])
    update_square = jnp.stack(
        [jnp.sum(update * update, axis=tuple(range(1, update.ndim))) for update in updates]
    )
    update_square = lax.psum(update_square, ("dp", "tensor"))
    ratio = jnp.sqrt(weight_square) / jnp.sqrt(update_square)
    outputs = [hidden, grad_rows, grad_norm]
    for kind_at in range(4):
        master = masters[kind_at]
        scaled = ratio[kind_at].reshape((-1,) + (1,) * (master.ndim - 1))
        outputs += [
            moments[kind_at][0],
            moments[kind_at][1],
            master - matrix_rate * scaled * updates[kind_at],
        ]
    small_first_new, small_second_new, small_direction = adam_parts(
        small_grad, small_first, small_second, factor
    )
    outputs += [small_first_new, small_second_new, small_params - vector_rate * small_direction]
    return tuple(outputs)


def solution(mesh):
    placed = (
        P("dp", None),
        P("dp", None),
        P("dp"),
        P(None, "dp", None, "tensor"),
        P(None, "dp", "tensor"),
        P(None, "dp", "tensor"),
        P(None, "dp", "tensor"),
        P(),
        P(None, "dp", None, "tensor"),
        P(None, "dp", None, "tensor"),
        P(None, "dp", "tensor"),
        P(None, "dp", "tensor"),
        P(None, "dp", "tensor"),
        P(None, "dp", "tensor"),
        P(None, "dp", "tensor"),
        P(None, "dp", "tensor"),
        P(),
        P(),
    )
    return jax.shard_map(
        local,
        mesh=mesh,
        in_specs=placed,
        out_specs=(
            P("dp", None),
            P("dp", None),
            P(),
            P(None, "dp", None, "tensor"),
            P(None, "dp", None, "tensor"),
            P(None, "dp", None, "tensor"),
            P(None, "dp", "tensor"),
            P(None, "dp", "tensor"),
            P(None, "dp", "tensor"),
            P(None, "dp", "tensor"),
            P(None, "dp", "tensor"),
            P(None, "dp", "tensor"),
            P(None, "dp", "tensor"),
            P(None, "dp", "tensor"),
            P(None, "dp", "tensor"),
            P(),
            P(),
            P(),
        ),
        check_vma=False,
    )
```

profile of v0, /device:TPU:0, one launch (start us, length us, event | category | flops | bytes accessed | tf_op | source)
XLA Modules:
  0.0 1741.2 jit_solution(10675762374318251473)
XLA Ops:
  13.1 72.2 %all-gather.5.cloned.1.call-done = bf16[2,768,3,384]{3,1,2,0:T(8,128)(2,1)} async-done(((bf16[2,48,3,384]{3,1,2,0:T(8,128)(2,1)}), bf16[2,768,3,384]{3,1,2,0:T(8,128)(2,1)}) %all-gather.5.cloned.1.call-update) | async-done | bytes 3538960 | tf_op jit(solution)/shard_map/all_gather | solution.py:137
  103.5 11.4 while.54
  116.8 26.5 %all-gather.7.cloned.1.call-done = bf16[2,768,384]{2,1,0:T(8,128)(2,1)} async-done(((bf16[2,48,384]{2,1,0:T(8,128)(2,1)}), bf16[2,768,384]{2,1,0:T(8,128)(2,1)}) %all-gather.7.cloned.1.call-update) | async-done | bytes 1179664 | tf_op jit(solution)/shard_map/all_gather | solution.py:138
  150.6 15.8 all-reduce.13.cloned.1.call-done
  169.4 82.1 %all-gather.9.cloned.1.call-done = bf16[2,768,1536]{2,1,0:T(8,128)(2,1)} async-done(((bf16[2,48,1536]{2,1,0:T(8,128)(2,1)}), bf16[2,768,1536]{2,1,0:T(8,128)(2,1)}) %all-gather.9.cloned.1.call-update) | async-done | bytes 4718608 | tf_op jit(solution)/shard_map/all_gather | solution.py:139
  251.5 20.8 %multiply_convert_fusion.1 = (bf16[1024,1536]{1,0:T(8,128)(2,1)}, f32[1024,1536]{1,0:T(8,128)}, f32[1024,1536]{1,0:T(8,128)}) fusion(f32[1536]{0:T(1024)S(1)} %dynamic-slice_reduce_fusion.5, bf16[2,768,1536]{2,1,0:T(8,128)(2,1)} %all-gather.9.cloned.1.call-done, f32[768]{0:T(1024)S(1)} %get-tuple-element.431, f32[768]{0:T(1024)S(1)} %get-tuple-element.432, ...), kind=kOutput, calls=%fused_computation.155 | convolution fusion | flops 2526806016 | bytes 21257216 | tf_op jit(solution)/shard_map/td,df->tf/dot_general | solution.py:190
  272.3 61.6 %all-gather.11.cloned.1.call-done = bf16[2,768,1536]{2,1,0:T(8,128)(2,1)} async-done(((bf16[2,48,1536]{2,1,0:T(8,128)(2,1)}), bf16[2,768,1536]{2,1,0:T(8,128)(2,1)}) %all-gather.11.cloned.1.call-update) | async-done | bytes 4718608 | tf_op jit(solution)/shard_map/all_gather | solution.py:140
  333.9 6.4 fusion.151
  340.5 19.1 %all-reduce.15.cloned.1.call-done = bf16[1024,768]{1,0:T(8,128)(2,1)} async-done(((bf16[1024,768]{1,0:T(8,128)(2,1)}), bf16[1024,768]{1,0:T(8,128)(2,1)}) %all-reduce.15.cloned.1.call-update) | async-done | bytes 1572880 | tf_op jit(solution)/shard_map/psum | solution.py:194
  380.8 14.3 while.55
  400.4 21.7 %all-reduce.17.cloned.1.call-done = bf16[1024,768]{1,0:T(8,128)(2,1)} async-done(((bf16[1024,768]{1,0:T(8,128)(2,1)}), bf16[1024,768]{1,0:T(8,128)(2,1)}) %all-reduce.17.cloned.1.call-update) | async-done | bytes 1572880 | tf_op jit(solution)/shard_map/psum | solution.py:181
  426.5 18.6 %multiply_convert_fusion = (bf16[1024,1536]{1,0:T(8,128)(2,1)S(1)}, f32[1024,1536]{1,0:T(8,128)}, f32[1024,1536]{1,0:T(8,128)}) fusion(f32[1536]{0:T(1024)S(1)} %dynamic-slice_reduce_fusion.4, bf16[2,768,1536]{2,1,0:T(8,128)(2,1)S(1)} %bitcast.417, f32[1024,768]{1,0:T(8,128)S(1)} %get-tuple-element.545, f32[768]{0:T(1024)S(1)} %copy-done.104, ...), kind=kOutput, calls=%fused_computation.142 | convolution fusion | flops 2523660288 | bytes 21258240 | tf_op jit(solution)/shard_map/td,df->tf/dot_general | solution.py:190
  452.2 21.7 %all-reduce.19.cloned.1.call-done = bf16[1024,768]{1,0:T(8,128)(2,1)} async-done(((bf16[1024,768]{1,0:T(8,128)(2,1)}), bf16[1024,768]{1,0:T(8,128)(2,1)}) %all-reduce.19.cloned.1.call-update) | async-done | bytes 1572880 | tf_op jit(solution)/shard_map/psum | solution.py:194
  484.4 9.5 fusion.211
  503.6 8.0 convolution_bitcast_fusion.2
  511.6 9.5 all-reduce.21.cloned.1.call-done
  541.2 36.4 %while.56 = (s32[]{:T(128)}, bf16[2,512,6,64]{1,3,2,0:T(8,128)(2,1)}, bf16[2,512,6,64]{1,3,2,0:T(8,128)(2,1)}, f32[2,512,6,64]{1,3,2,0:T(8,128)}, f32[2,6,512,51...) while((s32[]{:T(128)}, ...), condition=%wide.region_27.28_spmd, body=%wide.region_25.27_spmd.sunk | while | flops 1227224064 | bytes 94064864 | solution.py:276
  592.2 5.6 bitcast_convert_fusion.1
  598.0 7.9 convolution_bitcast_fusion
  613.1 6.5 all-reduce.23.cloned.1.call-done
  627.1 9.6 fusion.212
  647.8 7.4 pad_maximum_fusion.1
  676.7 54.2 %while.57 = (s32[]{:T(128)}, bf16[2,512,6,64]{1,3,2,0:T(8,128)(2,1)}, bf16[2,512,6,64]{1,3,2,0:T(8,128)(2,1)}, f32[2,512,6,64]{1,3,2,0:T(8,128)}, bf16[2,512,6,6...) while((s32[]{:T(128)}, ...), condition=%wide.region_36.37_spmd, body=%wide.region_34.36_spmd.sunk | while | flops 1222512128 | bytes 87736576 | solution.py:276
  681.9 7.6 fusion.310
  689.5 7.8 fusion.311
  709.0 7.6 fusion.310
  716.6 7.8 fusion.311
  745.3 8.5 pad_maximum_fusion
  772.1 736.8 %all-reduce.31.cloned.1.call-done = (f32[2,768,3,384]{3,1,2,0:T(8,128)}, f32[2,768,384]{2,1,0:T(8,128)}, f32[2,768,1536]{2,1,0:T(8,128)}, f32[2,768,1536]{2,1,0:T(8,128)}) async-done(((f32[2,768,3,384]{3,1,2,0:T(8,128)}, f32[2,768,384]{2,1,0:T(8,128)}, f32[2,768,1536]{2,1,0:T(8,128)}, f32[2,768,1536]{2,1,0:T(8,128)}), (f32[2,768,3,384]{3,1,2,0:T(8,128)}, f32[2,768,384]{2,1,0:T(8,128)}, ...) | async-done | bytes 28311568 | tf_op jit(solution)/shard_map/psum | solution.py:323
  1518.5 114.0 %all-reduce.29.cloned.1.call-done = f32[2,8448]{1,0:T(2,128)} async-done(((f32[2,8448]{1,0:T(2,128)}), f32[2,8448]{1,0:T(2,128)}) %all-reduce.29.cloned.1.call-update) | async-done | bytes 67600 | tf_op jit(solution)/shard_map/psum | solution.py:337
  1634.1 42.6 %psum.124 = f32[]{:T(128)} all-reduce(f32[]{:T(128)S(6)} %add.424), channel_id=1, replica_groups=mesh['dp'=16,'tensor'=2] {'dp','tensor'}, use_global_device_ids=true, to_apply=%region_46.47 | all-reduce | flops 1 | bytes 8 | tf_op jit(solution)/shard_map/psum | solution.py:337
  1687.8 39.3 %all-reduce = (f32[4,2]{1,0:T(4,128)S(1)}, f32[4,2]{1,0:T(4,128)S(1)}) all-reduce(f32[4,2]{1,0:T(4,128)S(1)} %pad_maximum_fusion.12, f32[4,2]{1,0:T(4,128)S(1)} %pad_maximum_fusion.11), channel_id=1, replica_groups=mesh['dp'=16,'tensor'=2] {'dp','tensor'}, use_global_device_ids=true, to_apply=%region_74.75 | all-reduce | flops 16 | bytes 128 | tf_op jit(solution)/shard_map/psum | solution.py:353
  (558 shorter events, 316.6 us)
Async XLA Ops:
  7.2 78.1 %all-gather.5.cloned.1.call-start = ((), (), s32[]{:S(2)}) async-start(), calls=%async_computation | async-start | bytes 3760128 | tf_op jit(solution)/shard_map/all_gather | solution.py:137
  9.0 134.3 %all-gather.7.cloned.1.call-start = ((), (), s32[]{:S(2)}) async-start(), calls=%async_computation.1 | async-start | bytes 1253376 | tf_op jit(solution)/shard_map/all_gather | solution.py:138
  10.6 155.7 %all-reduce.13.cloned.1.call-start = ((), (), s32[]{:S(2)}) async-start(), calls=%async_computation.2 | async-start | bytes 3145728 | tf_op jit(solution)/shard_map/psum | solution.py:181
  12.2 347.3 %copy-start.73 = (f32[768]{0:T(1024)}, f32[768]{0:T(1024)S(1)}, u32[]{:S(2)}) copy-start(f32[768]{0:T(1024)S(1)} %get-tuple-element.433) | copy-start | bytes 9220
  12.2 347.3 %copy-start.82 = (f32[768]{0:T(1024)}, f32[768]{0:T(1024)S(1)}, u32[]{:S(2)}) copy-start(f32[768]{0:T(1024)S(1)} %get-tuple-element.432) | copy-start | bytes 9220
  12.2 347.3 %copy-start.100 = (f32[768]{0:T(1024)}, f32[768]{0:T(1024)S(1)}, u32[]{:S(2)}) copy-start(f32[768]{0:T(1024)S(1)} %get-tuple-element.431) | copy-start | bytes 9220
  12.2 409.8 %copy-start.86 = (f32[768]{0:T(1024)}, f32[768]{0:T(1024)S(1)}, u32[]{:S(2)}) copy-start(f32[768]{0:T(1024)S(1)} %get-tuple-element.429) | copy-start | bytes 9220
  12.2 409.8 %copy-start.102 = (f32[768]{0:T(1024)}, f32[768]{0:T(1024)S(1)}, u32[]{:S(2)}) copy-start(f32[768]{0:T(1024)S(1)} %get-tuple-element.428) | copy-start | bytes 9220
  146.9 104.6 %all-gather.9.cloned.1.call-start = ((), (), s32[]{:S(2)}) async-start(), calls=%async_computation.3 | async-start | bytes 5013504 | tf_op jit(solution)/shard_map/all_gather | solution.py:139
  148.8 185.2 %all-gather.11.cloned.1.call-start = ((), (), s32[]{:S(2)}) async-start(), calls=%async_computation.4 | async-start | bytes 5013504 | tf_op jit(solution)/shard_map/all_gather | solution.py:140
  149.6 209.9 %all-reduce.15.cloned.1.call-start = ((), (), s32[]{:S(2)}) async-start(), calls=%async_computation.5 | async-start | bytes 3145728 | tf_op jit(solution)/shard_map/psum | solution.py:194
  150.5 100.9 %copy-start.116 = (f32[1536]{0:T(1024)}, f32[1536]{0:T(1024)S(1)}, u32[]{:S(2)}) copy-start(f32[1536]{0:T(1024)S(1)} %dynamic-slice_reduce_fusion.5) | copy-start | bytes 18436
  168.5 191.1 %copy-start.76 = (f32[1024]{0:T(1024)}, f32[1024]{0:T(1024)S(1)}, u32[]{:S(2)}) copy-start(f32[1024]{0:T(1024)S(1)} %broadcast_multiply_fusion.3) | copy-start | bytes 12292
  169.4 102.9 %copy-start.92 = (f32[1024]{0:T(1024)}, f32[1024]{0:T(1024)S(1)}, u32[]{:S(2)}) copy-start(f32[1024]{0:T(1024)S(1)} %multiply_reduce_fusion.13) | copy-start | bytes 12292
  169.4 190.2 %copy-start.84 = (f32[1024]{0:T(1024)}, f32[1024]{0:T(1024)S(1)}, u32[]{:S(2)}) copy-start(f32[1024]{0:T(1024)S(1)} %fusion.167) | copy-start | bytes 12292
  340.4 81.7 %all-reduce.17.cloned.1.call-start = ((), (), s32[]{:S(2)}) async-start(), calls=%async_computation.6 | async-start | bytes 3145728 | tf_op jit(solution)/shard_map/psum | solution.py:181
  363.2 58.9 %copy-start.78 = (f32[1024]{0:T(1024)}, f32[1024]{0:T(1024)S(1)}, u32[]{:S(2)}) copy-start(f32[1024]{0:T(1024)S(1)} %broadcast_multiply_fusion.2) | copy-start | bytes 12292
  363.7 58.4 %copy-start.89 = (f32[1024]{0:T(1024)}, f32[1024]{0:T(1024)S(1)}, u32[]{:S(2)}) copy-start(f32[1024]{0:T(1024)S(1)} %fusion.168) | copy-start | bytes 12292
  400.3 73.6 %all-reduce.19.cloned.1.call-start = ((), (), s32[]{:S(2)}) async-start(), calls=%async_computation.7 | async-start | bytes 3145728 | tf_op jit(solution)/shard_map/psum | solution.py:194
  452.2 68.9 %all-reduce.21.cloned.1.call-start = ((), (), s32[]{:S(2)}) async-start(), calls=%async_computation.8 | async-start | bytes 3145728 | tf_op jit(solution)/shard_map/psum | solution.py:246
  499.3 120.3 %all-reduce.23.cloned.1.call-start = ((), (), s32[]{:S(2)}) async-start(), calls=%async_computation.9 | async-start | bytes 3145728 | tf_op jit(solution)/shard_map/psum | solution.py:293
  597.9 65.9 %all-reduce.25.cloned.1.call-start = ((), (), s32[]{:S(2)}) async-start(), calls=%async_computation.10 | async-start | bytes 3145728 | tf_op jit(solution)/shard_map/psum | solution.py:246
  642.1 125.4 %all-reduce.27.cloned.1.call-start = ((), (), s32[]{:S(2)}) async-start(), calls=%async_computation.11 | async-start | bytes 3145728 | tf_op jit(solution)/shard_map/psum | solution.py:293
  745.0 763.9 %all-reduce.31.cloned.1.call-start = ((), (), s32[]{:S(2)}) async-start(), calls=%async_computation.13 | async-start | bytes 56623104 | tf_op jit(solution)/shard_map/psum | solution.py:323
  763.9 868.6 %all-reduce.29.cloned.1.call-start = ((), (), s32[]{:S(2)}) async-start(), calls=%async_computation.12 | async-start | bytes 135168 | tf_op jit(solution)/shard_map/psum | solution.py:337
  767.5 910.6 %copy-start.47 = (f32[2,48,384]{2,1,0:T(8,128)S(1)}, f32[2,48,384]{2,1,0:T(8,128)}, u32[]{:S(2)}) copy-start(f32[2,48,384]{2,1,0:T(8,128)} %param.30) | copy-start | bytes 442372
  771.2 908.8 %copy-start.34 = (f32[2,48,1536]{2,1,0:T(8,128)S(1)}, f32[2,48,1536]{2,1,0:T(8,128)}, u32[]{:S(2)}) copy-start(f32[2,48,1536]{2,1,0:T(8,128)} %param.31) | copy-start | bytes 1769476
  771.2 908.8 %copy-start.66 = (f32[2,48,1536]{2,1,0:T(8,128)S(1)}, f32[2,48,1536]{2,1,0:T(8,128)}, u32[]{:S(2)}) copy-start(f32[2,48,1536]{2,1,0:T(8,128)} %param.38) | copy-start | bytes 1769476
  1508.9 173.1 %copy-start.33 = (f32[2,48,1536]{2,1,0:T(8,128)S(1)}, f32[2,48,1536]{2,1,0:T(8,128)}, u32[]{:S(2)}) copy-start(f32[2,48,1536]{2,1,0:T(8,128)} %param.32) | copy-start | bytes 1769476
  1682.0 47.4 %copy-start.42 = (f32[2,48,1536]{2,1,0:T(8,128)}, f32[2,48,1536]{2,1,0:T(8,128)S(1)}, u32[]{:S(2)}) copy-start(f32[2,48,1536]{2,1,0:T(8,128)S(1)} %get-tuple-element.528) | copy-start | bytes 1769476
  1682.0 47.4 %copy-start.43 = (f32[2,48,1536]{2,1,0:T(8,128)}, f32[2,48,1536]{2,1,0:T(8,128)S(1)}, u32[]{:S(2)}) copy-start(f32[2,48,1536]{2,1,0:T(8,128)S(1)} %get-tuple-element.529) | copy-start | bytes 1769476
  1685.2 45.4 %copy-start.44 = (f32[2,48,1536]{2,1,0:T(8,128)}, f32[2,48,1536]{2,1,0:T(8,128)S(1)}, u32[]{:S(2)}) copy-start(f32[2,48,1536]{2,1,0:T(8,128)S(1)} %get-tuple-element.530) | copy-start | bytes 1769476
  (127 other events, 746.6 us)
Sparse Core Ops, SparseCore 0:
  11.3 73.9 all-gather.4
  88.5 54.6 all-gather.6
  147.0 19.2 all-reduce.12
  169.8 81.6 all-gather.8
  255.0 78.9 all-gather.10
  340.5 19.0 all-reduce.14
  400.5 21.5 all-reduce.16
  452.3 21.5 all-reduce.18
  499.5 21.5 all-reduce.20
  598.0 21.5 all-reduce.22
  642.2 21.5 all-reduce.24
  745.1 21.5 all-reduce.26
  773.2 735.7 all-reduce.30
  1515.9 116.6 all-reduce.28
where the time goes:
time: 1750 us; the launch traced here: 1740 us
  waiting for transfers between devices  1190 us (68%)
  matrix products  238 us (14%)
  other arithmetic  120 us (7%)
  local copies, waits for them, and re-layouts  86.9 us (5%)
  blocking collectives  81.9 us (5%)
  between operations  20.9 us (1%)
    psum x1, waiting for transfers between devices, local(): lax.psum((big_totals[0], big_totals[1], big_totals[2], big_totals[3]), 'dp')  737 us
    psum x1, waiting for transfers between devices, local(): lax.psum((square_part, weight_square, small_partial), ('dp', 'tensor'))  114 us
    all_gather x1, waiting for transfers between devices, local(): lax.all_gather(up_weight.astype(jnp.bfloat16), 'dp', axis=1, tiled=True)  82.1 us
    all_gather x1, waiting for transfers between devices, local(): lax.all_gather(proj_weight.astype(jnp.bfloat16), 'dp', axis=1, tiled=True)  72.2 us
    all_gather x1, waiting for transfers between devices, local(): lax.all_gather(down_weight.astype(jnp.bfloat16), 'dp', axis=1, tiled=True)  61.6 us
    psum x1, blocking collectives, local(): lax.psum((square_part, weight_square, small_partial), ('dp', 'tensor'))  42.6 us
    psum x2, waiting for transfers between devices, local(): lax.psum(jnp.einsum('tf,df->td', act_low, down_full[layer_at], preferred_...  40.7 us
    dot_general x2, matrix products, local(): jnp.einsum('td,df->tf', first_low, up_full[layer_at], preferred_element_t...  39.4 us
  transfers between devices with their start and end apart: 14, of which 13 were waited for; matrix products, arithmetic and copies ran while one was open for 8% of the time, Pallas kernels for 0%

commit v1 on v0

--- a/solution.py
+++ b/solution.py
@@ -137,7 +137,12 @@
         lax.all_gather(proj_weight.astype(jnp.bfloat16), "dp", axis=1, tiled=True),
         lax.all_gather(out_weight.astype(jnp.bfloat16), "dp", axis=1, tiled=True),
         lax.all_gather(up_weight.astype(jnp.bfloat16), "dp", axis=1, tiled=True),
-        lax.all_gather(down_weight.astype(jnp.bfloat16), "dp", axis=1, tiled=True),
+        jnp.concatenate(
+            lax.all_to_all(
+                jnp.stack([down_weight.astype(jnp.bfloat16)] * lax.axis_size("dp")), "dp", 0, 0
+            ),
+            axis=1,
+        ),
     )
     positions = jnp.arange(seq_len)
     key_valid = positions[None, :] < lengths[:, None]

time: 1750 us -> 1730 us (0.989)
    all_to_all x0 -> x1, waiting for transfers between devices: none -> 91.1 us  [local(): lax.all_to_all(jnp.stack([down_weight.astype(jnp.bfloat16)] * lax.axis_si...]
    all_gather x1 -> x0, waiting for transfers between devices: 61.6 us -> none  [local(): lax.all_gather(down_weight.astype(jnp.bfloat16), 'dp', axis=1, tiled=True)]
    all_gather x1, waiting for transfers between devices: 82.1 us -> 36.2 us  [local(): lax.all_gather(up_weight.astype(jnp.bfloat16), 'dp', axis=1, tiled=True)]
  transfers between devices with their start and end apart: 14 -> 14, of which waited for: 13 -> 14; matrix products, arithmetic and copies ran while one was open for 8% -> 7% of each run, Pallas kernels for 0% -> 0%
where the time goes in v1:
time: 1730 us; the launch traced here: 1720 us
  waiting for transfers between devices  1180 us (68%)
  matrix products  230 us (13%)
  other arithmetic  120 us (7%)
  blocking collectives  81.9 us (5%)
  local copies, waits for them, and re-layouts  80.6 us (5%)
  between operations  21 us (1%)
    psum x1, waiting for transfers between devices, local(): lax.psum((big_totals[0], big_totals[1], big_totals[2], big_totals[3]), 'dp')  737 us
    psum x1, waiting for transfers between devices, local(): lax.psum((square_part, weight_square, small_partial), ('dp', 'tensor'))  114 us
    all_to_all x1, waiting for transfers between devices, local(): lax.all_to_all(jnp.stack([down_weight.astype(jnp.bfloat16)] * lax.axis_si...  91.1 us
    all_gather x1, waiting for transfers between devices, local(): lax.all_gather(proj_weight.astype(jnp.bfloat16), 'dp', axis=1, tiled=True)  72.2 us
    psum x2, waiting for transfers between devices, local(): lax.psum(jnp.einsum('tf,df->td', act_low, down_full[layer_at], preferred_...  45.5 us
    psum x1, blocking collectives, local(): lax.psum((square_part, weight_square, small_partial), ('dp', 'tensor'))  42.6 us
    psum x1, blocking collectives, local(): update_square = lax.psum(update_square, ('dp', 'tensor'))  39.3 us
    dot_general x2, matrix products, local(): jnp.einsum('td,df->tf', first_low, up_full[layer_at], preferred_element_t...  39.2 us
  transfers between devices with their start and end apart: 14, of which 14 were waited for; matrix products, arithmetic and copies ran while one was open for 7% of the time, Pallas kernels for 0%

profile of v1, /device:TPU:0, one launch (start us, length us, event | category | flops | bytes accessed | tf_op | source)
XLA Modules:
  0.0 1721.5 jit_solution(15477596357881578237)
XLA Ops:
  13.1 72.2 %all-gather.4.cloned.1.call-done = bf16[2,768,3,384]{3,1,2,0:T(8,128)(2,1)} async-done(((bf16[2,48,3,384]{3,1,2,0:T(8,128)(2,1)}), bf16[2,768,3,384]{3,1,2,0:T(8,128)(2,1)}) %all-gather.4.cloned.1.call-update) | async-done | bytes 3538960 | tf_op jit(solution)/shard_map/all_gather | solution.py:137
  85.3 5.6 fusion.206
  100.1 11.4 while.54
  112.5 30.8 %all-gather.6.cloned.1.call-done = bf16[2,768,384]{2,1,0:T(8,128)(2,1)} async-done(((bf16[2,48,384]{2,1,0:T(8,128)(2,1)}), bf16[2,768,384]{2,1,0:T(8,128)(2,1)}) %all-gather.6.cloned.1.call-update) | async-done | bytes 1179664 | tf_op jit(solution)/shard_map/all_gather | solution.py:138
  156.0 10.0 all-reduce.13.cloned.1.call-done
  169.0 91.1 %all-to-all-done = bf16[16,2,48,1536]{3,2,1,0:T(8,128)(2,1)} async-done(((bf16[16,2,48,1536]{3,2,1,0:T(8,128)(2,1)}), bf16[16,2,48,1536]{3,2,1,0:T(8,128)(2,1)}, u32[]{:S(2)}, u32[]{:S(2)}) %all-to-all-start) | async-done | bytes 4718624 | tf_op jit(solution)/shard_map/all_to_all | solution.py:141
  265.7 36.2 %all-gather.8.cloned.1.call-done = bf16[2,768,1536]{2,1,0:T(8,128)(2,1)} async-done(((bf16[2,48,1536]{2,1,0:T(8,128)(2,1)}), bf16[2,768,1536]{2,1,0:T(8,128)(2,1)}) %all-gather.8.cloned.1.call-update) | async-done | bytes 4718608 | tf_op jit(solution)/shard_map/all_gather | solution.py:139
  301.9 20.5 %multiply_convert_fusion.1 = (bf16[1024,1536]{1,0:T(8,128)(2,1)S(1)}, f32[1024,1536]{1,0:T(8,128)}, f32[1024,1536]{1,0:T(8,128)}) fusion(f32[1536]{0:T(1024)S(1)} %dynamic-slice_reduce_fusion.5, bf16[2,768,1536]{2,1,0:T(8,128)(2,1)} %all-gather.8.cloned.1.call-done, f32[768]{0:T(1024)S(1)} %get-tuple-element.431, f32[768]{0:T(1024)S(1)} %get-tuple-element.432, ...), kind=kOutput, calls=%fused_computation.155 | convolution fusion | flops 2526806016 | bytes 21257216 | tf_op jit(solution)/shard_map/td,df->tf/dot_general | solution.py:195
  328.4 23.8 %all-reduce.15.cloned.1.call-done = bf16[1024,768]{1,0:T(8,128)(2,1)} async-done(((bf16[1024,768]{1,0:T(8,128)(2,1)}), bf16[1024,768]{1,0:T(8,128)(2,1)}) %all-reduce.15.cloned.1.call-update) | async-done | bytes 1572880 | tf_op jit(solution)/shard_map/psum | solution.py:199
  373.1 13.5 while.55
  392.3 21.6 %all-reduce.17.cloned.1.call-done = bf16[1024,768]{1,0:T(8,128)(2,1)} async-done(((bf16[1024,768]{1,0:T(8,128)(2,1)}), bf16[1024,768]{1,0:T(8,128)(2,1)}) %all-reduce.17.cloned.1.call-update) | async-done | bytes 1572880 | tf_op jit(solution)/shard_map/psum | solution.py:186
  418.4 18.7 %multiply_convert_fusion = (bf16[1024,1536]{1,0:T(8,128)(2,1)S(1)}, f32[1024,1536]{1,0:T(8,128)}, f32[1024,1536]{1,0:T(8,128)}) fusion(f32[1536]{0:T(1024)S(1)} %dynamic-slice_reduce_fusion.4, bf16[2,768,1536]{2,1,0:T(8,128)(2,1)S(1)} %bitcast.408, f32[1024,768]{1,0:T(8,128)S(1)} %get-tuple-element.545, f32[768]{0:T(1024)S(1)} %copy-done.100, ...), kind=kOutput, calls=%fused_computation.142 | convolution fusion | flops 2523660288 | bytes 21258240 | tf_op jit(solution)/shard_map/td,df->tf/dot_general | solution.py:195
  442.5 21.7 %all-reduce.19.cloned.1.call-done = bf16[1024,768]{1,0:T(8,128)(2,1)} async-done(((bf16[1024,768]{1,0:T(8,128)(2,1)}), bf16[1024,768]{1,0:T(8,128)(2,1)}) %all-reduce.19.cloned.1.call-update) | async-done | bytes 1572880 | tf_op jit(solution)/shard_map/psum | solution.py:199
  474.9 8.6 fusion.208
  491.7 8.0 convolution_bitcast_fusion.2
  499.7 10.9 all-reduce.21.cloned.1.call-done
  527.1 36.1 %while.56 = (s32[]{:T(128)}, bf16[2,512,6,64]{1,3,2,0:T(8,128)(2,1)}, bf16[2,512,6,64]{1,3,2,0:T(8,128)(2,1)}, f32[2,512,6,64]{1,3,2,0:T(8,128)}, f32[2,6,512,51...) while((s32[]{:T(128)}, ...), condition=%wide.region_27.28_spmd, body=%wide.region_25.27_spmd.sunk | while | flops 1227224064 | bytes 90919112 | solution.py:281
  578.7 7.8 convolution_bitcast_fusion
  593.9 6.0 all-reduce.23.cloned.1.call-done
  607.4 8.9 fusion.209
  621.8 5.6 convolution_bitcast_fusion.1
  627.5 7.4 pad_maximum_fusion.1
  656.2 54.4 %while.57 = (s32[]{:T(128)}, bf16[2,512,6,64]{1,3,2,0:T(8,128)(2,1)}, bf16[2,512,6,64]{1,3,2,0:T(8,128)(2,1)}, f32[2,512,6,64]{1,3,2,0:T(8,128)}, bf16[2,512,6,6...) while((s32[]{:T(128)}, ...), condition=%wide.region_36.37_spmd, body=%wide.region_34.36_spmd.sunk | while | flops 1222512128 | bytes 87736576 | solution.py:281
  661.4 7.6 fusion.311
  669.0 7.8 fusion.312
  688.5 7.6 fusion.311
  696.1 7.8 fusion.312
  724.7 8.5 pad_maximum_fusion
  751.4 736.7 %all-reduce.31.cloned.1.call-done = (f32[2,768,3,384]{3,1,2,0:T(8,128)}, f32[2,768,384]{2,1,0:T(8,128)}, f32[2,768,1536]{2,1,0:T(8,128)}, f32[2,768,1536]{2,1,0:T(8,128)}) async-done(((f32[2,768,3,384]{3,1,2,0:T(8,128)}, f32[2,768,384]{2,1,0:T(8,128)}, f32[2,768,1536]{2,1,0:T(8,128)}, f32[2,768,1536]{2,1,0:T(8,128)}), (f32[2,768,3,384]{3,1,2,0:T(8,128)}, f32[2,768,384]{2,1,0:T(8,128)}, ...) | async-done | bytes 28311568 | tf_op jit(solution)/shard_map/psum | solution.py:328
  1497.7 114.2 %all-reduce.29.cloned.1.call-done = f32[2,8448]{1,0:T(2,128)} async-done(((f32[2,8448]{1,0:T(2,128)}), f32[2,8448]{1,0:T(2,128)}) %all-reduce.29.cloned.1.call-update) | async-done | bytes 67600 | tf_op jit(solution)/shard_map/psum | solution.py:342
  1613.5 42.6 %psum.124 = f32[]{:T(128)} all-reduce(f32[]{:T(128)S(6)} %add.424), channel_id=1, replica_groups=mesh['dp'=16,'tensor'=2] {'dp','tensor'}, use_global_device_ids=true, to_apply=%region_46.47 | all-reduce | flops 1 | bytes 8 | tf_op jit(solution)/shard_map/psum | solution.py:342
  1667.0 39.3 %all-reduce = (f32[4,2]{1,0:T(4,128)S(1)}, f32[4,2]{1,0:T(4,128)S(1)}) all-reduce(f32[4,2]{1,0:T(4,128)S(1)} %pad_maximum_fusion.12, f32[4,2]{1,0:T(4,128)S(1)} %pad_maximum_fusion.11), channel_id=1, replica_groups=mesh['dp'=16,'tensor'=2] {'dp','tensor'}, use_global_device_ids=true, to_apply=%region_74.75 | all-reduce | flops 16 | bytes 128 | tf_op jit(solution)/shard_map/psum | solution.py:358
  (547 shorter events, 312.0 us)
Async XLA Ops:
  7.2 78.1 %all-gather.4.cloned.1.call-start = ((), (), s32[]{:S(2)}) async-start(), calls=%async_computation.1 | async-start | bytes 3760128 | tf_op jit(solution)/shard_map/all_gather | solution.py:137
  9.0 134.3 %all-gather.6.cloned.1.call-start = ((), (), s32[]{:S(2)}) async-start(), calls=%async_computation.2 | async-start | bytes 1253376 | tf_op jit(solution)/shard_map/all_gather | solution.py:138
  10.6 155.4 %all-reduce.13.cloned.1.call-start = ((), (), s32[]{:S(2)}) async-start(), calls=%async_computation.3 | async-start | bytes 3145728 | tf_op jit(solution)/shard_map/psum | solution.py:186
  12.2 340.0 %copy-start.71 = (f32[768]{0:T(1024)}, f32[768]{0:T(1024)S(1)}, u32[]{:S(2)}) copy-start(f32[768]{0:T(1024)S(1)} %get-tuple-element.433) | copy-start | bytes 9220
  12.2 340.0 %copy-start.81 = (f32[768]{0:T(1024)}, f32[768]{0:T(1024)S(1)}, u32[]{:S(2)}) copy-start(f32[768]{0:T(1024)S(1)} %get-tuple-element.432) | copy-start | bytes 9220
  12.2 340.0 %copy-start.96 = (f32[768]{0:T(1024)}, f32[768]{0:T(1024)S(1)}, u32[]{:S(2)}) copy-start(f32[768]{0:T(1024)S(1)} %get-tuple-element.431) | copy-start | bytes 9220
  12.2 401.7 %copy-start.85 = (f32[768]{0:T(1024)}, f32[768]{0:T(1024)S(1)}, u32[]{:S(2)}) copy-start(f32[768]{0:T(1024)S(1)} %get-tuple-element.429) | copy-start | bytes 9220
  12.2 401.7 %copy-start.98 = (f32[768]{0:T(1024)}, f32[768]{0:T(1024)S(1)}, u32[]{:S(2)}) copy-start(f32[768]{0:T(1024)S(1)} %get-tuple-element.428) | copy-start | bytes 9220
  149.3 110.9 %all-to-all-start = ((bf16[16,2,48,1536]{3,2,1,0:T(8,128)(2,1)}), bf16[16,2,48,1536]{3,2,1,0:T(8,128)(2,1)}, u32[]{:S(2)}, u32[]{:S(2)}) async-start(bf16[16,2,48,1536]{3,2,1,0:T(8,128)(2,1)} %stack.102), calls=%async_computation | async-start | bytes 9437184 | tf_op jit(solution)/shard_map/all_to_all | solution.py:141
  154.0 147.9 %all-gather.8.cloned.1.call-start = ((), (), s32[]{:S(2)}) async-start(), calls=%async_computation.4 | async-start | bytes 5013504 | tf_op jit(solution)/shard_map/all_gather | solution.py:139
  154.8 197.4 %all-reduce.15.cloned.1.call-start = ((), (), s32[]{:S(2)}) async-start(), calls=%async_computation.5 | async-start | bytes 3145728 | tf_op jit(solution)/shard_map/psum | solution.py:199
  156.0 145.9 %copy-start.112 = (f32[1536]{0:T(1024)}, f32[1536]{0:T(1024)S(1)}, u32[]{:S(2)}) copy-start(f32[1536]{0:T(1024)S(1)} %dynamic-slice_reduce_fusion.5) | copy-start | bytes 18436
  168.1 184.1 %copy-start.75 = (f32[1024]{0:T(1024)}, f32[1024]{0:T(1024)S(1)}, u32[]{:S(2)}) copy-start(f32[1024]{0:T(1024)S(1)} %broadcast_multiply_fusion.3) | copy-start | bytes 12292
  169.0 96.7 %copy-start.91 = (f32[1024]{0:T(1024)}, f32[1024]{0:T(1024)S(1)}, u32[]{:S(2)}) copy-start(f32[1024]{0:T(1024)S(1)} %multiply_reduce_fusion.13) | copy-start | bytes 12292
  169.0 183.2 %copy-start.83 = (f32[1024]{0:T(1024)}, f32[1024]{0:T(1024)S(1)}, u32[]{:S(2)}) copy-start(f32[1024]{0:T(1024)S(1)} %fusion.161) | copy-start | bytes 12292
  327.9 86.0 %all-reduce.17.cloned.1.call-start = ((), (), s32[]{:S(2)}) async-start(), calls=%async_computation.6 | async-start | bytes 3145728 | tf_op jit(solution)/shard_map/psum | solution.py:186
  355.6 58.3 %copy-start.77 = (f32[1024]{0:T(1024)}, f32[1024]{0:T(1024)S(1)}, u32[]{:S(2)}) copy-start(f32[1024]{0:T(1024)S(1)} %broadcast_multiply_fusion.2) | copy-start | bytes 12292
  356.1 57.8 %copy-start.88 = (f32[1024]{0:T(1024)}, f32[1024]{0:T(1024)S(1)}, u32[]{:S(2)}) copy-start(f32[1024]{0:T(1024)S(1)} %fusion.162) | copy-start | bytes 12292
  392.2 72.0 %all-reduce.19.cloned.1.call-start = ((), (), s32[]{:S(2)}) async-start(), calls=%async_computation.7 | async-start | bytes 3145728 | tf_op jit(solution)/shard_map/psum | solution.py:199
  442.4 68.2 %all-reduce.21.cloned.1.call-start = ((), (), s32[]{:S(2)}) async-start(), calls=%async_computation.8 | async-start | bytes 3145728 | tf_op jit(solution)/shard_map/psum | solution.py:251
  488.9 111.0 %all-reduce.23.cloned.1.call-start = ((), (), s32[]{:S(2)}) async-start(), calls=%async_computation.9 | async-start | bytes 3145728 | tf_op jit(solution)/shard_map/psum | solution.py:298
  578.2 65.3 %all-reduce.25.cloned.1.call-start = ((), (), s32[]{:S(2)}) async-start(), calls=%async_computation.10 | async-start | bytes 3145728 | tf_op jit(solution)/shard_map/psum | solution.py:251
  621.7 124.3 %all-reduce.27.cloned.1.call-start = ((), (), s32[]{:S(2)}) async-start(), calls=%async_computation.11 | async-start | bytes 3145728 | tf_op jit(solution)/shard_map/psum | solution.py:298
  724.3 763.8 %all-reduce.31.cloned.1.call-start = ((), (), s32[]{:S(2)}) async-start(), calls=%async_computation.13 | async-start | bytes 56623104 | tf_op jit(solution)/shard_map/psum | solution.py:328
  742.8 869.1 %all-reduce.29.cloned.1.call-start = ((), (), s32[]{:S(2)}) async-start(), calls=%async_computation.12 | async-start | bytes 135168 | tf_op jit(solution)/shard_map/psum | solution.py:342
  744.7 912.8 %copy-start.51 = (f32[2,48,384]{2,1,0:T(8,128)S(1)}, f32[2,48,384]{2,1,0:T(8,128)}, u32[]{:S(2)}) copy-start(f32[2,48,384]{2,1,0:T(8,128)} %param.30) | copy-start | bytes 442372
  744.7 912.8 %copy-start.73 = (f32[2,48,384]{2,1,0:T(8,128)S(1)}, f32[2,48,384]{2,1,0:T(8,128)}, u32[]{:S(2)}) copy-start(f32[2,48,384]{2,1,0:T(8,128)} %param.36) | copy-start | bytes 442372
  744.7 912.8 %copy-start.74 = (f32[2,48,384]{2,1,0:T(8,128)S(1)}, f32[2,48,384]{2,1,0:T(8,128)}, u32[]{:S(2)}) copy-start(f32[2,48,384]{2,1,0:T(8,128)} %param.37) | copy-start | bytes 442372
  750.6 908.7 %copy-start.34 = (f32[2,48,1536]{2,1,0:T(8,128)S(1)}, f32[2,48,1536]{2,1,0:T(8,128)}, u32[]{:S(2)}) copy-start(f32[2,48,1536]{2,1,0:T(8,128)} %param.31) | copy-start | bytes 1769476
  1488.1 173.3 %copy-start.32 = (f32[2,48,1536]{2,1,0:T(8,128)S(1)}, f32[2,48,1536]{2,1,0:T(8,128)}, u32[]{:S(2)}) copy-start(f32[2,48,1536]{2,1,0:T(8,128)} %param.32) | copy-start | bytes 1769476
  1661.4 47.4 %copy-start.43 = (f32[2,48,1536]{2,1,0:T(8,128)}, f32[2,48,1536]{2,1,0:T(8,128)S(1)}, u32[]{:S(2)}) copy-start(f32[2,48,1536]{2,1,0:T(8,128)S(1)} %get-tuple-element.528) | copy-start | bytes 1769476
  1661.4 47.4 %copy-start.44 = (f32[2,48,1536]{2,1,0:T(8,128)}, f32[2,48,1536]{2,1,0:T(8,128)S(1)}, u32[]{:S(2)}) copy-start(f32[2,48,1536]{2,1,0:T(8,128)S(1)} %get-tuple-element.529) | copy-start | bytes 1769476
  (121 other events, 805.6 us)
Sparse Core Ops, SparseCore 0:
  11.3 73.9 all-gather.3
  88.5 54.6 all-gather.5
  146.7 19.2 all-reduce.12
  169.4 132.4 all-gather.7
  328.0 24.1 all-reduce.14
  392.3 21.5 all-reduce.16
  442.5 21.5 all-reduce.18
  489.0 21.5 all-reduce.20
  578.3 21.5 all-reduce.22
  621.9 21.5 all-reduce.24
  724.5 21.5 all-reduce.26
  752.4 735.7 all-reduce.30
  1495.2 116.6 all-reduce.28
